TPU v7x, 32 devices: a whole 2x2x4 slice. The times are simulated.
32 devices in a mesh: comp: 4 (over y, core), tile: 8 (over z, x).
Axes of the slice: x: 2, y: 2, z: 4, core: 2. Of those that a mesh axis runs over, the one named last changes fastest.
Arguments:
- state: float32 [2, 8, 256, 4096], P(None, None, 'comp', 'tile'), may hold values from -6 to 6
- courant: float32 [8, 256], P(None, 'comp'), may hold values from -0.9 to 0.9
- mixing: float32 [7, 256], P(None, 'comp'), may hold values from 0.05 to 0.24
- exchange_coef: float32 [256, 4096], P('comp', 'tile'), may hold values from 0.2 to 0.8
- sea_mask: int32 [256, 4096], P('comp', 'tile'), may hold values 0 or 1
- margin_count: int32 [4, 8, 3, 4], P('comp', 'tile'), may hold values from 0 to 4096, as said below
- margin_row: int32 [4, 8, 3, 4, 4096], P('comp', 'tile'), may hold values from 0 to 63
- margin_col: int32 [4, 8, 3, 4, 4096], P('comp', 'tile'), may hold values from 0 to 511, as said below
- margin_weight: float32 [4, 8, 3, 4, 4096], P('comp', 'tile'), may hold values from 0.05 to 0.6
Outputs:
- new_state: float32 [2, 8, 256, 4096], P(None, None, 'comp', 'tile')
- partner_surface: float32 [2, 256, 4096], P(None, 'comp', 'tile')
Inputs may be any that keep to these rules, and one draw needn't show every extreme that they name: margin_count[g, t, o, h] equals margin_count[h, (t + o - 1) mod 8, 2 - o, g], and row r of the one list is the same margin as row r of the other. Only pairs of one atmosphere device (comp index below 3) and one ocean device have rows: an atmosphere device couples with the three ocean devices at tile offsets -1, 0 and 1, an ocean device with the atmosphere devices at those offsets; every such pair has at least 3584 rows. `margin_col`: for list index o = 0 (partner to the west) the columns lie below 128, for o = 2 (partner to the east) at 384 or above.
All inputs are finite; a program needn't handle non-finite values. No bound on the sum of `sea_mask` on one device may be relied on, other than what follows from the above.
Results may differ from a plain program's by a relative error of at most 0.0003.
Values sent between devices are 32-bit elements; how exact they have to be, the bound alone decides.
A program may use at most 64 MiB of HBM per device.

v0:
```python
import jax
import jax.numpy as jnp
from jax import lax
from jax.sharding import PartitionSpec as P

SUBSTEPS = 2


def with_halo(block, sides, width):
    for axis, dim in sides:
        count = lax.axis_size(axis)
        forward = [(i, i + 1) for i in range(count - 1)]
        forward.append((count - 1, 0))
        backward = [(target, source) for source, target in forward]
        low = lax.ppermute(
            lax.slice_in_dim(block, block.shape[dim] - width, None, axis=dim), axis, forward
        )
        high = lax.ppermute(lax.slice_in_dim(block, 0, width, axis=dim), axis, backward)
        block = jnp.concatenate([low, block, high], axis=dim)
    return block


def transport(padded, speed):
    left = padded[..., :-2]
    middle = padded[..., 1:-1]
    right = padded[..., 2:]
    return (
        middle - 0.5 * speed * (right - left) + 0.5 * speed * speed * (right - 2.0 * middle + left)
    )


def vertical_mix(field, coeff):
    jump_up = field[:, 1:] - field[:, :-1]
    flux = coeff[None, :, :, None] * jump_up
    empty = jnp.zeros_like(flux[:, :1])
    upper = jnp.concatenate([flux, empty], axis=1)
    lower = jnp.concatenate([empty, flux], axis=1)
    return field + upper - lower


def shards(
    state,
    courant,
    mixing,
    exchange_coef,
    sea_mask,
    margin_count,
    margin_row,
    margin_col,
    margin_weight,
):
    field_count, level_count, row_count, col_count = state.shape
    slot_count = margin_row.shape[-1]
    comp_peers = margin_row.shape[3]
    list_count = 3 * comp_peers
    tile_total = lax.axis_size("tile")
    tile_here = lax.axis_index("tile")
    surface_rows = state[:, 0].reshape(field_count * row_count, col_count)
    row_lists = margin_row.reshape(list_count, slot_count)
    col_lists = margin_col.reshape(list_count, slot_count)
    counts = margin_count.reshape(list_count)
    row_iota = jnp.arange(row_count, dtype=jnp.int32)[:, None]
    col_iota = jnp.arange(col_count, dtype=jnp.int32)[:, None]
    slot_iota = jnp.arange(slot_count, dtype=jnp.int32)

    def pick_list(carry, parts):
        row_list, col_list, count_one = parts
        col_table = (col_iota == col_list[None, :]).astype(jnp.float32)
        picked = jnp.dot(
            surface_rows,
            col_table,
            precision=lax.Precision.HIGHEST,
            preferred_element_type=jnp.float32,
        )
        picked = picked.reshape(field_count, row_count, slot_count)
        row_match = row_iota == row_list[None, :]
        values = jnp.sum(jnp.where(row_match[None], picked, 0.0), axis=1)
        values = jnp.where((slot_iota < count_one)[None, :], values, 0.0)
        return (carry, values)

    unused, picked_all = lax.scan(pick_list, 0, (row_lists, col_lists, counts))
    outgoing = jnp.transpose(
        picked_all.reshape(3, comp_peers, field_count, slot_count), (2, 0, 1, 3)
    )
    partner_tiles = (tile_here + jnp.arange(3, dtype=jnp.int32) - 1) % tile_total
    tile_table = partner_tiles[:, None] == jnp.arange(tile_total, dtype=jnp.int32)[None, :]
    spread = jnp.where(tile_table[None, :, None, :, None], outgoing[:, :, :, None, :], 0.0)
    blocks = jnp.sum(spread, axis=1).reshape(field_count, comp_peers * tile_total, slot_count)
    arrived = lax.all_to_all(blocks, ("comp", "tile"), split_axis=1, concat_axis=1, tiled=True)
    arrived = arrived.reshape(field_count, comp_peers, tile_total, slot_count)
    chosen = jnp.where(tile_table[None, :, None, :, None], arrived[:, None], 0.0)
    incoming = jnp.sum(chosen, axis=3)
    speed = courant[:, :, None]
    field = state
    padded = with_halo(field, (("tile", 3),), SUBSTEPS)
    for step in range(SUBSTEPS):
        padded = vertical_mix(transport(padded, speed), mixing)
    field = padded
    weights = margin_weight.reshape(3, comp_peers, slot_count)
    terms = jnp.transpose(
        (incoming * weights[None]).reshape(field_count, list_count, slot_count), (1, 0, 2)
    )

    def land_list(total, parts):
        row_list, col_list, term_one = parts
        col_table = (col_iota == col_list[None, :]).astype(jnp.float32)
        row_match = row_iota == row_list[None, :]
        spread = jnp.where(row_match[None], term_one[:, None, :], 0.0).reshape(
            field_count * row_count, slot_count
        )
        landed = lax.dot_general(
            spread,
            col_table,
            (((1,), (1,)), ((), ())),
            precision=lax.Precision.HIGHEST,
            preferred_element_type=jnp.float32,
        )
        return (total + landed, 0)

    start_total = jnp.zeros((field_count * row_count, col_count), jnp.float32)
    partner, unused_two = lax.scan(land_list, start_total, (row_lists, col_lists, terms))
    partner = partner.reshape(field_count, row_count, col_count)
    ocean = lax.axis_index("comp") == lax.axis_size("comp") - 1
    rate = exchange_coef * sea_mask.astype(jnp.float32)
    first_own = field[0, 0]
    second_own = field[1, 0]
    first_far = partner[0]
    second_far = partner[1]
    new_first = first_own + rate * (first_far - first_own)
    air_second = second_own + rate * (1.2 * first_far - 0.3 * second_far - second_own)
    sea_second = second_own + rate * (1.2 * first_own - second_far)
    new_second = jnp.where(ocean, sea_second, air_second)
    field = field.at[:, 0].set(jnp.stack([new_first, new_second]))
    return (field, partner)


def solution(mesh):
    in_specs = (
        P(None, None, "comp", "tile"),
        P(None, "comp"),
        P(None, "comp"),
        P("comp", "tile"),
        P("comp", "tile"),
        P("comp", "tile", None, None),
        P("comp", "tile", None, None, None),
        P("comp", "tile", None, None, None),
        P("comp", "tile", None, None, None),
    )
    out_specs = (P(None, None, "comp", "tile"), P(None, "comp", "tile"))
    return jax.shard_map(shards, mesh=mesh, in_specs=in_specs, out_specs=out_specs, check_vma=False)
```

profile of v0, /device:TPU:0, one launch (start us, length us, event | category | flops | bytes accessed | tf_op | source)
XLA Modules:
  0.0 178.6 jit_solution(16265510379821095748)
XLA Ops:
  0.7 2.4 %fusion.21 = (f32[2,8,64,2]{3,2,1,0:T(8,128)}, f32[2,8,64,2]{3,2,1,0:T(8,128)}) fusion(f32[2,8,64,512]{3,2,1,0:T(8,128)} %param.15), kind=kLoop, calls=%fused_computation.54 | loop fusion | bytes 32768 | tf_op jit(solution)/shard_map/slice | solution.py:16
  3.1 6.0 %collective-permute-start.1 = (f32[2,8,64,2]{3,2,1,0:T(8,128)}, f32[2,8,64,2]{3,2,1,0:T(8,128)}, u32[]{:S(2)}, u32[]{:S(2)}) collective-permute-start(f32[2,8,64,2]{3,2,1,0:T(8,128)} %get-tuple-element.167), channel_id=1, source_target_pairs={{1,0},{2,1},{3,2},{4,3},{5,4},{6,5},{7,6},{0,7},{9,8},{10,9},{11,1... | collective-permute-start | bytes 24584 | tf_op jit(solution)/shard_map/ppermute | solution.py:18
  9.4 54.5 %while.23 = (s32[]{:T(128)}, f32[12,2,4096]{2,1,0:T(2,128)S(1)}, s32[12]{0:T(128)S(1)}, s32[12,4096]{1,0:T(8,128)S(1)}, s32[12,4096]{1,0:T(8,128)S(1)}, /*index=5*/f32[128,512]{1,0:T(8,128)S(1)}, s32[]{:T(128)}) while((s32[]{:T(128)}, f32[12,2,4096]{2,1,0:T(2,128)S(1)}, s32[12]{0:T(128)S(1)}, s32[12,4096]{1,0:T(8,128)S(1)}, ...), condition=%wide.region_2.3_spmd.clone, body=%wide.region_0.2_spmd.clone.sunk | while | flops 3224637440 | bytes 991333 | solution.py:81
  9.5 3.1 %select_reduce_fusion.4 = f32[2,4096]{1,0:T(2,128)S(1)} fusion(pred[64,4096]{1,0:T(8,128)(4,1)S(1)} %iota_compare_fusion.14, f32[128,512]{1,0:T(8,128)S(1)} %get-tuple-element.265, s32[4096]{0:T(1024)S(1)} %bitcast.76), kind=kOutput, calls=%fused_computation.8.clone.1 | convolution fusion | flops 3224363008 | bytes 573440 | tf_op jit(solution)/shard_map/while/body/eval_jaxpr/dot_general | solution.py:69
  12.7 0.6 dynamic_slice.43
  14.1 3.1 %select_reduce_fusion.4 = f32[2,4096]{1,0:T(2,128)S(1)} fusion(pred[64,4096]{1,0:T(8,128)(4,1)S(1)} %iota_compare_fusion.14, f32[128,512]{1,0:T(8,128)S(1)} %get-tuple-element.265, s32[4096]{0:T(1024)S(1)} %bitcast.76), kind=kOutput, calls=%fused_computation.8.clone.1 | convolution fusion | flops 3224363008 | bytes 573440 | tf_op jit(solution)/shard_map/while/body/eval_jaxpr/dot_general | solution.py:69
  18.6 3.1 %select_reduce_fusion.4 = f32[2,4096]{1,0:T(2,128)S(1)} fusion(pred[64,4096]{1,0:T(8,128)(4,1)S(1)} %iota_compare_fusion.14, f32[128,512]{1,0:T(8,128)S(1)} %get-tuple-element.265, s32[4096]{0:T(1024)S(1)} %bitcast.76), kind=kOutput, calls=%fused_computation.8.clone.1 | convolution fusion | flops 3224363008 | bytes 573440 | tf_op jit(solution)/shard_map/while/body/eval_jaxpr/dot_general | solution.py:69
  21.8 0.6 dynamic_slice.43
  23.2 3.1 %select_reduce_fusion.4 = f32[2,4096]{1,0:T(2,128)S(1)} fusion(pred[64,4096]{1,0:T(8,128)(4,1)S(1)} %iota_compare_fusion.14, f32[128,512]{1,0:T(8,128)S(1)} %get-tuple-element.265, s32[4096]{0:T(1024)S(1)} %bitcast.76), kind=kOutput, calls=%fused_computation.8.clone.1 | convolution fusion | flops 3224363008 | bytes 573440 | tf_op jit(solution)/shard_map/while/body/eval_jaxpr/dot_general | solution.py:69
  26.3 0.6 dynamic_slice.43
  27.7 3.1 %select_reduce_fusion.4 = f32[2,4096]{1,0:T(2,128)S(1)} fusion(pred[64,4096]{1,0:T(8,128)(4,1)S(1)} %iota_compare_fusion.14, f32[128,512]{1,0:T(8,128)S(1)} %get-tuple-element.265, s32[4096]{0:T(1024)S(1)} %bitcast.76), kind=kOutput, calls=%fused_computation.8.clone.1 | convolution fusion | flops 3224363008 | bytes 573440 | tf_op jit(solution)/shard_map/while/body/eval_jaxpr/dot_general | solution.py:69
  30.8 0.6 dynamic_slice.43
  32.3 3.1 %select_reduce_fusion.4 = f32[2,4096]{1,0:T(2,128)S(1)} fusion(pred[64,4096]{1,0:T(8,128)(4,1)S(1)} %iota_compare_fusion.14, f32[128,512]{1,0:T(8,128)S(1)} %get-tuple-element.265, s32[4096]{0:T(1024)S(1)} %bitcast.76), kind=kOutput, calls=%fused_computation.8.clone.1 | convolution fusion | flops 3224363008 | bytes 573440 | tf_op jit(solution)/shard_map/while/body/eval_jaxpr/dot_general | solution.py:69
  35.4 0.6 dynamic_slice.43
  36.8 3.1 %select_reduce_fusion.4 = f32[2,4096]{1,0:T(2,128)S(1)} fusion(pred[64,4096]{1,0:T(8,128)(4,1)S(1)} %iota_compare_fusion.14, f32[128,512]{1,0:T(8,128)S(1)} %get-tuple-element.265, s32[4096]{0:T(1024)S(1)} %bitcast.76), kind=kOutput, calls=%fused_computation.8.clone.1 | convolution fusion | flops 3224363008 | bytes 573440 | tf_op jit(solution)/shard_map/while/body/eval_jaxpr/dot_general | solution.py:69
  39.9 0.6 dynamic_slice.43
  41.3 3.1 %select_reduce_fusion.4 = f32[2,4096]{1,0:T(2,128)S(1)} fusion(pred[64,4096]{1,0:T(8,128)(4,1)S(1)} %iota_compare_fusion.14, f32[128,512]{1,0:T(8,128)S(1)} %get-tuple-element.265, s32[4096]{0:T(1024)S(1)} %bitcast.76), kind=kOutput, calls=%fused_computation.8.clone.1 | convolution fusion | flops 3224363008 | bytes 573440 | tf_op jit(solution)/shard_map/while/body/eval_jaxpr/dot_general | solution.py:69
  44.5 0.6 dynamic_slice.43
  45.9 3.1 %select_reduce_fusion.4 = f32[2,4096]{1,0:T(2,128)S(1)} fusion(pred[64,4096]{1,0:T(8,128)(4,1)S(1)} %iota_compare_fusion.14, f32[128,512]{1,0:T(8,128)S(1)} %get-tuple-element.265, s32[4096]{0:T(1024)S(1)} %bitcast.76), kind=kOutput, calls=%fused_computation.8.clone.1 | convolution fusion | flops 3224363008 | bytes 573440 | tf_op jit(solution)/shard_map/while/body/eval_jaxpr/dot_general | solution.py:69
  50.4 3.1 %select_reduce_fusion.4 = f32[2,4096]{1,0:T(2,128)S(1)} fusion(pred[64,4096]{1,0:T(8,128)(4,1)S(1)} %iota_compare_fusion.14, f32[128,512]{1,0:T(8,128)S(1)} %get-tuple-element.265, s32[4096]{0:T(1024)S(1)} %bitcast.76), kind=kOutput, calls=%fused_computation.8.clone.1 | convolution fusion | flops 3224363008 | bytes 573440 | tf_op jit(solution)/shard_map/while/body/eval_jaxpr/dot_general | solution.py:69
  53.6 0.6 dynamic_slice.43
  55.0 3.1 %select_reduce_fusion.4 = f32[2,4096]{1,0:T(2,128)S(1)} fusion(pred[64,4096]{1,0:T(8,128)(4,1)S(1)} %iota_compare_fusion.14, f32[128,512]{1,0:T(8,128)S(1)} %get-tuple-element.265, s32[4096]{0:T(1024)S(1)} %bitcast.76), kind=kOutput, calls=%fused_computation.8.clone.1 | convolution fusion | flops 3224363008 | bytes 573440 | tf_op jit(solution)/shard_map/while/body/eval_jaxpr/dot_general | solution.py:69
  58.1 0.6 dynamic_slice.43
  59.5 3.1 %select_reduce_fusion.4 = f32[2,4096]{1,0:T(2,128)S(1)} fusion(pred[64,4096]{1,0:T(8,128)(4,1)S(1)} %iota_compare_fusion.14, f32[128,512]{1,0:T(8,128)S(1)} %get-tuple-element.265, s32[4096]{0:T(1024)S(1)} %bitcast.76), kind=kOutput, calls=%fused_computation.8.clone.1 | convolution fusion | flops 3224363008 | bytes 573440 | tf_op jit(solution)/shard_map/while/body/eval_jaxpr/dot_general | solution.py:69
  62.6 0.6 dynamic_slice.43
  63.9 0.7 copy-done.1
  65.3 1.8 %copy.20 = f32[2,32,4096]{2,0,1:T(2,128)} copy(f32[2,32,4096]{2,1,0:T(8,128)S(1)} %bitcast.71) | data formatting | bytes 2097152 | tf_op jit(solution)/shard_map/reshape | solution.py:88
  67.1 6.2 %all-to-all-start = ((f32[2,32,4096]{2,0,1:T(2,128)}), f32[2,32,4096]{2,0,1:T(2,128)S(1)}, u32[]{:S(2)}, u32[]{:S(2)}) async-start(f32[2,32,4096]{2,0,1:T(2,128)} %copy.20), calls=%async_computation | async-start | bytes 2097152 | tf_op jit(solution)/shard_map/all_to_all | solution.py:89
  73.4 1.6 constant_dynamic-update-slice_fusion.1
  75.0 1.0 mul.126
  76.0 1.9 %constant_dynamic-update-slice_fusion = f32[2,8,64,514]{3,2,1,0:T(8,128)} fusion(f32[2,8,64,514]{3,2,1,0:T(8,128)} %constant_dynamic-update-slice_fusion.1, f32[2,8,64,2]{3,2,1,0:T(8,128)} %collective-permute-done.1), kind=kLoop, calls=%fused_computation.45 | loop fusion | bytes 1048576 | tf_op jit(solution)/shard_map/concatenate | solution.py:19
  78.0 3.8 %multiply_add_fusion = f32[2,8,64,514]{3,2,1,0:T(8,128)S(1)} fusion(f32[2,8,64,514]{3,2,1,0:T(8,128)} %constant_dynamic-update-slice_fusion, f32[2,8,64,2]{3,2,1,0:T(8,128)} %collective-permute-done.1, f32[2,8,64,512]{3,2,1,0:T(8,128)S(1)} %copy-done, f32[2,8,64,2]{3,2,1,0:T(8,128)} %collective-permute-done, f32[8,64]{1,0:T(8,128)S(1)} %get-tuple-element.169, ...), kind=kLoop, calls=%fused_computation.30 | loop fusion | flops 5789696 | bytes 6328320 | tf_op jit(solution)/shard_map/add | solution.py:28
  82.4 1.3 multiply_add_fusion.1
  84.0 2.6 %pad_subtract_fusion.1 = f32[2,8,64,512]{3,2,1,0:T(8,128)} fusion(f32[2,7,64,512]{3,2,1,0:T(8,128)S(1)} %fusion.17, f32[8,64]{1,0:T(8,128)S(1)} %get-tuple-element.169, f32[2,8,64,514]{3,2,1,0:T(8,128)S(1)} %pad_subtract_fusion, f32[8,64]{1,0:T(8,128)S(1)} %get-tuple-element.168), kind=kLoop, calls=%fused_computation.33 | loop fusion | flops 5242880 | bytes 10227712 | tf_op jit(solution)/shard_map/sub | solution.py:38
  86.7 14.0 %all-to-all-done = f32[2,32,4096]{2,0,1:T(2,128)S(1)} async-done(((f32[2,32,4096]{2,0,1:T(2,128)}), f32[2,32,4096]{2,0,1:T(2,128)S(1)}, u32[]{:S(2)}, u32[]{:S(2)}) %all-to-all-start) | async-done | bytes 1048608 | tf_op jit(solution)/shard_map/all_to_all | solution.py:89
  100.6 0.6 copy.21
  101.3 1.0 select_reduce_fusion.1
  102.9 73.8 %while.24 = (s32[]{:T(128)}, f32[128,512]{1,0:T(8,128)S(1)}, s32[12,4096]{1,0:T(8,128)}, f32[12,2,4096]{2,1,0:T(2,128)S(1)}, s32[12,4096]{1,0:T(8,128)}, /*index=5*/s32[]{:T(128)}, s32[]{:T(128)}) while((s32[]{:T(128)}, f32[128,512]{1,0:T(8,128)S(1)}, s32[12,4096]{1,0:T(8,128)}, f32[12,2,4096]{2,1,0:T(2,128)S(1)}, ...), condition=%wide.region_6.7_spmd.clone, body=%wide.region_5.6_spmd.clone.sunk | while | flops 3224240128 | bytes 5439583 | solution.py:121
  102.9 1.1 constant_dynamic-slice_fusion.7
  104.3 4.7 %fusion.31 = f32[128,512]{1,0:T(8,128)S(1)} fusion(f32[128,4096]{1,0:T(8,128)S(1)} %bitcast.68, s32[4096]{0:T(1024)S(1)} %bitcast.75, f32[128,512]{1,0:T(8,128)S(1)} %get-tuple-element.275, pred[]{:T(512)S(6)} %compare.17), kind=kOutput, calls=%fused_computation.18.clone.1 | convolution fusion | flops 3223453696 | bytes 2637825 | tf_op jit(solution)/shard_map/while/body/eval_jaxpr/dot_general | solution.py:111
  109.1 1.0 constant_dynamic-slice_fusion.7
  110.5 4.7 %fusion.31 = f32[128,512]{1,0:T(8,128)S(1)} fusion(f32[128,4096]{1,0:T(8,128)S(1)} %bitcast.68, s32[4096]{0:T(1024)S(1)} %bitcast.75, f32[128,512]{1,0:T(8,128)S(1)} %get-tuple-element.275, pred[]{:T(512)S(6)} %compare.17), kind=kOutput, calls=%fused_computation.18.clone.1 | convolution fusion | flops 3223453696 | bytes 2637825 | tf_op jit(solution)/shard_map/while/body/eval_jaxpr/dot_general | solution.py:111
  115.2 1.0 constant_dynamic-slice_fusion.7
  116.6 4.7 %fusion.31 = f32[128,512]{1,0:T(8,128)S(1)} fusion(f32[128,4096]{1,0:T(8,128)S(1)} %bitcast.68, s32[4096]{0:T(1024)S(1)} %bitcast.75, f32[128,512]{1,0:T(8,128)S(1)} %get-tuple-element.275, pred[]{:T(512)S(6)} %compare.17), kind=kOutput, calls=%fused_computation.18.clone.1 | convolution fusion | flops 3223453696 | bytes 2637825 | tf_op jit(solution)/shard_map/while/body/eval_jaxpr/dot_general | solution.py:111
  121.4 1.0 constant_dynamic-slice_fusion.7
  122.8 4.7 %fusion.31 = f32[128,512]{1,0:T(8,128)S(1)} fusion(f32[128,4096]{1,0:T(8,128)S(1)} %bitcast.68, s32[4096]{0:T(1024)S(1)} %bitcast.75, f32[128,512]{1,0:T(8,128)S(1)} %get-tuple-element.275, pred[]{:T(512)S(6)} %compare.17), kind=kOutput, calls=%fused_computation.18.clone.1 | convolution fusion | flops 3223453696 | bytes 2637825 | tf_op jit(solution)/shard_map/while/body/eval_jaxpr/dot_general | solution.py:111
  127.5 1.0 constant_dynamic-slice_fusion.7
  128.9 4.7 %fusion.31 = f32[128,512]{1,0:T(8,128)S(1)} fusion(f32[128,4096]{1,0:T(8,128)S(1)} %bitcast.68, s32[4096]{0:T(1024)S(1)} %bitcast.75, f32[128,512]{1,0:T(8,128)S(1)} %get-tuple-element.275, pred[]{:T(512)S(6)} %compare.17), kind=kOutput, calls=%fused_computation.18.clone.1 | convolution fusion | flops 3223453696 | bytes 2637825 | tf_op jit(solution)/shard_map/while/body/eval_jaxpr/dot_general | solution.py:111
  133.7 1.0 constant_dynamic-slice_fusion.7
  135.1 4.7 %fusion.31 = f32[128,512]{1,0:T(8,128)S(1)} fusion(f32[128,4096]{1,0:T(8,128)S(1)} %bitcast.68, s32[4096]{0:T(1024)S(1)} %bitcast.75, f32[128,512]{1,0:T(8,128)S(1)} %get-tuple-element.275, pred[]{:T(512)S(6)} %compare.17), kind=kOutput, calls=%fused_computation.18.clone.1 | convolution fusion | flops 3223453696 | bytes 2637825 | tf_op jit(solution)/shard_map/while/body/eval_jaxpr/dot_general | solution.py:111
  139.8 1.0 constant_dynamic-slice_fusion.7
  141.2 4.7 %fusion.31 = f32[128,512]{1,0:T(8,128)S(1)} fusion(f32[128,4096]{1,0:T(8,128)S(1)} %bitcast.68, s32[4096]{0:T(1024)S(1)} %bitcast.75, f32[128,512]{1,0:T(8,128)S(1)} %get-tuple-element.275, pred[]{:T(512)S(6)} %compare.17), kind=kOutput, calls=%fused_computation.18.clone.1 | convolution fusion | flops 3223453696 | bytes 2637825 | tf_op jit(solution)/shard_map/while/body/eval_jaxpr/dot_general | solution.py:111
  146.0 1.0 constant_dynamic-slice_fusion.7
  147.3 4.7 %fusion.31 = f32[128,512]{1,0:T(8,128)S(1)} fusion(f32[128,4096]{1,0:T(8,128)S(1)} %bitcast.68, s32[4096]{0:T(1024)S(1)} %bitcast.75, f32[128,512]{1,0:T(8,128)S(1)} %get-tuple-element.275, pred[]{:T(512)S(6)} %compare.17), kind=kOutput, calls=%fused_computation.18.clone.1 | convolution fusion | flops 3223453696 | bytes 2637825 | tf_op jit(solution)/shard_map/while/body/eval_jaxpr/dot_general | solution.py:111
  152.1 1.0 constant_dynamic-slice_fusion.7
  153.5 4.7 %fusion.31 = f32[128,512]{1,0:T(8,128)S(1)} fusion(f32[128,4096]{1,0:T(8,128)S(1)} %bitcast.68, s32[4096]{0:T(1024)S(1)} %bitcast.75, f32[128,512]{1,0:T(8,128)S(1)} %get-tuple-element.275, pred[]{:T(512)S(6)} %compare.17), kind=kOutput, calls=%fused_computation.18.clone.1 | convolution fusion | flops 3223453696 | bytes 2637825 | tf_op jit(solution)/shard_map/while/body/eval_jaxpr/dot_general | solution.py:111
  158.3 1.0 constant_dynamic-slice_fusion.7
  159.6 4.7 %fusion.31 = f32[128,512]{1,0:T(8,128)S(1)} fusion(f32[128,4096]{1,0:T(8,128)S(1)} %bitcast.68, s32[4096]{0:T(1024)S(1)} %bitcast.75, f32[128,512]{1,0:T(8,128)S(1)} %get-tuple-element.275, pred[]{:T(512)S(6)} %compare.17), kind=kOutput, calls=%fused_computation.18.clone.1 | convolution fusion | flops 3223453696 | bytes 2637825 | tf_op jit(solution)/shard_map/while/body/eval_jaxpr/dot_general | solution.py:111
  164.4 1.0 constant_dynamic-slice_fusion.7
  165.8 4.7 %fusion.31 = f32[128,512]{1,0:T(8,128)S(1)} fusion(f32[128,4096]{1,0:T(8,128)S(1)} %bitcast.68, s32[4096]{0:T(1024)S(1)} %bitcast.75, f32[128,512]{1,0:T(8,128)S(1)} %get-tuple-element.275, pred[]{:T(512)S(6)} %compare.17), kind=kOutput, calls=%fused_computation.18.clone.1 | convolution fusion | flops 3223453696 | bytes 2637825 | tf_op jit(solution)/shard_map/while/body/eval_jaxpr/dot_general | solution.py:111
  170.6 1.0 constant_dynamic-slice_fusion.7
  171.9 4.7 %fusion.31 = f32[128,512]{1,0:T(8,128)S(1)} fusion(f32[128,4096]{1,0:T(8,128)S(1)} %bitcast.68, s32[4096]{0:T(1024)S(1)} %bitcast.75, f32[128,512]{1,0:T(8,128)S(1)} %get-tuple-element.275, pred[]{:T(512)S(6)} %compare.17), kind=kOutput, calls=%fused_computation.18.clone.1 | convolution fusion | flops 3223453696 | bytes 2637825 | tf_op jit(solution)/shard_map/while/body/eval_jaxpr/dot_general | solution.py:111
  176.7 1.1 add_bitcast_fusion
  177.9 0.7 fusion.18
  (130 shorter events, 17.2 us)
Async XLA Ops:
  0.6 8.7 %slice-start = ((f32[2,8,64,512]{3,2,1,0:T(8,128)}), f32[2,1,64,512]{3,2,1,0:T(8,128)S(1)}, s32[]{:S(2)}) async-start(f32[2,8,64,512]{3,2,1,0:T(8,128)} %param.15), calls=%async_computation.1 | async-start | bytes 524288 | tf_op jit(solution)/shard_map/slice | solution.py:58
  0.6 8.4 %copy-start.5 = (s32[1,1,3,4,4096]{4,3,2,1,0:T(4,128)S(1)}, s32[1,1,3,4,4096]{4,3,2,1,0:T(4,128)}, u32[]{:S(2)}) copy-start(s32[1,1,3,4,4096]{4,3,2,1,0:T(4,128)} %param.21) | copy-start | bytes 589828
  0.7 8.5 %copy-start.6 = (s32[1,1,3,4,4096]{4,3,2,1,0:T(4,128)S(1)}, s32[1,1,3,4,4096]{4,3,2,1,0:T(4,128)}, u32[]{:S(2)}) copy-start(s32[1,1,3,4,4096]{4,3,2,1,0:T(4,128)} %param.22) | copy-start | bytes 589828
  0.7 8.6 %copy-start.11 = (s32[1,1,3,4]{3,1,2,0:T(1,128)S(1)}, s32[1,1,3,4]{3,1,2,0:T(1,128)}, u32[]{:S(2)}) copy-start(s32[1,1,3,4]{3,1,2,0:T(1,128)} %param.20) | copy-start | bytes 148
  3.1 73.0 %collective-permute-start.1 = (f32[2,8,64,2]{3,2,1,0:T(8,128)}, f32[2,8,64,2]{3,2,1,0:T(8,128)}, u32[]{:S(2)}, u32[]{:S(2)}) collective-permute-start(f32[2,8,64,2]{3,2,1,0:T(8,128)} %get-tuple-element.167), channel_id=1, source_target_pairs={{1,0},{2,1},{3,2},{4,3},{5,4},{6,5},{7,6},{0,7},{9,8},{10,9},{11,1... | collective-permute-start | bytes 24584 | tf_op jit(solution)/shard_map/ppermute | solution.py:18
  9.1 68.9 %collective-permute-start = (f32[2,8,64,2]{3,2,1,0:T(8,128)}, f32[2,8,64,2]{3,2,1,0:T(8,128)}, u32[]{:S(2)}, u32[]{:S(2)}) collective-permute-start(f32[2,8,64,2]{3,2,1,0:T(8,128)} %get-tuple-element.166), channel_id=1, source_target_pairs={{0,1},{1,2},{2,3},{3,4},{4,5},{5,6},{6,7},{7,0},{8,9},{9,10},{10,1... | collective-permute-start | bytes 24584 | tf_op jit(solution)/shard_map/ppermute | solution.py:15
  63.9 0.7 copy-start.1
  63.9 1.4 copy-start.2
  65.3 8.1 %copy-start.10 = (f32[8,64]{1,0:T(8,128)S(1)}, f32[8,64]{1,0:T(8,128)}, u32[]{:S(2)}) copy-start(f32[8,64]{1,0:T(8,128)} %param.16) | copy-start | bytes 6148
  65.3 8.1 %copy-start = (f32[2,8,64,512]{3,2,1,0:T(8,128)S(1)}, f32[2,8,64,512]{3,2,1,0:T(8,128)}, u32[]{:S(2)}) copy-start(f32[2,8,64,512]{3,2,1,0:T(8,128)} %param.15) | copy-start | bytes 6291460
  67.1 33.5 %all-to-all-start = ((f32[2,32,4096]{2,0,1:T(2,128)}), f32[2,32,4096]{2,0,1:T(2,128)S(1)}, u32[]{:S(2)}, u32[]{:S(2)}) async-start(f32[2,32,4096]{2,0,1:T(2,128)} %copy.20), calls=%async_computation | async-start | bytes 2097152 | tf_op jit(solution)/shard_map/all_to_all | solution.py:89
  78.0 3.8 %copy-start.9 = (f32[7,64]{1,0:T(8,128)S(1)}, f32[7,64]{1,0:T(8,128)}, u32[]{:S(2)}) copy-start(f32[7,64]{1,0:T(8,128)} %param.17) | copy-start | bytes 5380
  101.2 1.6 copy-start.3
  102.8 73.9 %copy-start.7 = (f32[64,512]{1,0:T(8,128)S(1)}, f32[64,512]{1,0:T(8,128)}, u32[]{:S(2)}) copy-start(f32[64,512]{1,0:T(8,128)} %param.18) | copy-start | bytes 393220
  102.9 73.9 %copy-start.8 = (s32[64,512]{1,0:T(8,128)S(1)}, s32[64,512]{1,0:T(8,128)}, u32[]{:S(2)}) copy-start(s32[64,512]{1,0:T(8,128)} %param.19) | copy-start | bytes 393220
  176.7 1.9 %copy-start.4 = (f32[128,512]{1,0:T(8,128)}, f32[128,512]{1,0:T(8,128)S(1)}, u32[]{:S(2)}) copy-start(f32[128,512]{1,0:T(8,128)S(1)} %get-tuple-element.99) | copy-start | bytes 786436
where the time goes:
time: 179 us
  matrix products  94.5 us (53%)
  local copies, waits for them, and re-layouts  30.5 us (17%)
  other arithmetic  25.3 us (14%)
  waiting for transfers between devices  14 us (8%)
  starting transfers between devices  12.2 us (7%)
    dot_general x12, matrix products, land_list(): lax.dot_general(spread, col_table, (((1,), (1,)), ((), ())), precision=la...  56.9 us
    dot_general x12, matrix products, pick_list(): jnp.dot(surface_rows, col_table, precision=lax.Precision.HIGHEST, preferr...  37.6 us
    dynamic_slice x36, local copies, waits for them, and re-layouts, shards(): unused, picked_all = lax.scan(pick_list, 0, (row_lists, col_lists, counts))  19.5 us
    all_to_all x1, waiting for transfers between devices, shards(): lax.all_to_all(blocks, ('comp', 'tile'), split_axis=1, concat_axis=1, til...  14 us
    lt x12, other arithmetic, pick_list(): values = jnp.where((slot_iota < count_one)[None, :], values, 0.0)  6.79 us
    all_to_all x1, starting transfers between devices, shards(): lax.all_to_all(blocks, ('comp', 'tile'), split_axis=1, concat_axis=1, til...  6.22 us
    ppermute x1, starting transfers between devices, with_halo(): lax.ppermute(lax.slice_in_dim(block, 0, width, axis=dim), axis, backward)  6 us
    add x2, other arithmetic, transport(): middle - 0.5 * speed * (right - left)  5.15 us
  transfers between devices with their start and end apart: 3, of which 1 were waited for; matrix products, arithmetic and copies ran while one was open for 39% of the time, Pallas kernels for 0%

commit v1 on v0

--- a/solution.py
+++ b/solution.py
@@ -86,7 +86,15 @@
     tile_table = partner_tiles[:, None] == jnp.arange(tile_total, dtype=jnp.int32)[None, :]
     spread = jnp.where(tile_table[None, :, None, :, None], outgoing[:, :, :, None, :], 0.0)
     blocks = jnp.sum(spread, axis=1).reshape(field_count, comp_peers * tile_total, slot_count)
-    arrived = lax.all_to_all(blocks, ("comp", "tile"), split_axis=1, concat_axis=1, tiled=True)
+    arrived = jnp.concatenate(
+        lax.all_to_all(
+            jnp.stack(jnp.split(blocks, lax.axis_size(("comp", "tile")), axis=1)),
+            ("comp", "tile"),
+            0,
+            0,
+        ),
+        axis=1,
+    )
     arrived = arrived.reshape(field_count, comp_peers, tile_total, slot_count)
     chosen = jnp.where(tile_table[None, :, None, :, None], arrived[:, None], 0.0)
     incoming = jnp.sum(chosen, axis=3)

time: 179 us -> 200 us (1.12)
  local copies, waits for them, and re-layouts: 30.5 us -> 50.6 us
    unnamed x25 -> x56, local copies, waits for them, and re-layouts: 2.4 us -> 21.9 us
  transfers between devices with their start and end apart: 3 -> 3, of which waited for: 1 -> 1; matrix products, arithmetic and copies ran while one was open for 39% -> 45% of each run, Pallas kernels for 0% -> 0%
where the time goes in v1:
time: 200 us; the launch traced here: 199 us
  matrix products  94.5 us (47%)
  local copies, waits for them, and re-layouts  50.6 us (25%)
  other arithmetic  26 us (13%)
  waiting for transfers between devices  13.9 us (7%)
  starting transfers between devices  12.2 us (6%)
    dot_general x12, matrix products, land_list(): lax.dot_general(spread, col_table, (((1,), (1,)), ((), ())), precision=la...  56.9 us
    dot_general x12, matrix products, pick_list(): jnp.dot(surface_rows, col_table, precision=lax.Precision.HIGHEST, preferr...  37.6 us
    unnamed x56, local copies, waits for them, and re-layouts  21.9 us
    dynamic_slice x36, local copies, waits for them, and re-layouts, shards(): unused, picked_all = lax.scan(pick_list, 0, (row_lists, col_lists, counts))  20.2 us
    all_to_all x1, waiting for transfers between devices, shards(): lax.all_to_all(jnp.stack(jnp.split(blocks, lax.axis_size(('comp', 'tile')...  13.9 us
    lt x12, other arithmetic, pick_list(): values = jnp.where((slot_iota < count_one)[None, :], values, 0.0)  7.5 us
    all_to_all x1, starting transfers between devices, shards(): lax.all_to_all(jnp.stack(jnp.split(blocks, lax.axis_size(('comp', 'tile')...  6.22 us
    ppermute x1, starting transfers between devices, with_halo(): lax.ppermute(lax.slice_in_dim(block, 0, width, axis=dim), axis, backward)  6 us
  transfers between devices with their start and end apart: 3, of which 1 were waited for; matrix products, arithmetic and copies ran while one was open for 45% of the time, Pallas kernels for 0%

profile of v1, /device:TPU:0, one launch (start us, length us, event | category | flops | bytes accessed | tf_op | source)
XLA Modules:
  0.0 199.3 jit_solution(7464765532289910595)
XLA Ops:
  0.7 2.4 %fusion.21 = (f32[2,8,64,2]{3,2,1,0:T(8,128)}, f32[2,8,64,2]{3,2,1,0:T(8,128)}) fusion(f32[2,8,64,512]{3,2,1,0:T(8,128)} %param.15), kind=kLoop, calls=%fused_computation.118 | loop fusion | bytes 32768 | tf_op jit(solution)/shard_map/slice | solution.py:16
  3.1 6.0 %collective-permute-start.1 = (f32[2,8,64,2]{3,2,1,0:T(8,128)}, f32[2,8,64,2]{3,2,1,0:T(8,128)}, u32[]{:S(2)}, u32[]{:S(2)}) collective-permute-start(f32[2,8,64,2]{3,2,1,0:T(8,128)} %get-tuple-element.167), channel_id=1, source_target_pairs={{1,0},{2,1},{3,2},{4,3},{5,4},{6,5},{7,6},{0,7},{9,8},{10,9},{11,1... | collective-permute-start | bytes 24584 | tf_op jit(solution)/shard_map/ppermute | solution.py:18
  9.4 55.9 %while.23 = (s32[]{:T(128)}, f32[12,2,4096]{2,1,0:T(2,128)S(1)}, s32[12]{0:T(128)S(1)}, s32[12,4096]{1,0:T(8,128)S(1)}, s32[12,4096]{1,0:T(8,128)S(1)}, /*index=5*/f32[128,512]{1,0:T(8,128)S(1)}, s32[]{:T(128)}) while((s32[]{:T(128)}, f32[12,2,4096]{2,1,0:T(2,128)S(1)}, s32[12]{0:T(128)S(1)}, s32[12,4096]{1,0:T(8,128)S(1)}, ...), condition=%wide.region_2.3_spmd.clone, body=%wide.region_0.2_spmd.clone.sunk | while | flops 3224637440 | bytes 991341 | solution.py:81
  9.6 3.1 %select_reduce_fusion.4 = f32[2,4096]{1,0:T(2,128)S(1)} fusion(pred[64,4096]{1,0:T(8,128)(4,1)S(1)} %iota_compare_fusion.14, f32[128,512]{1,0:T(8,128)S(1)} %get-tuple-element.297, s32[4096]{0:T(1024)S(1)} %bitcast.207), kind=kOutput, calls=%fused_computation.8.clone.1 | convolution fusion | flops 3224363008 | bytes 573440 | tf_op jit(solution)/shard_map/while/body/eval_jaxpr/dot_general | solution.py:69
  12.7 0.7 dynamic_slice.43
  14.2 3.1 %select_reduce_fusion.4 = f32[2,4096]{1,0:T(2,128)S(1)} fusion(pred[64,4096]{1,0:T(8,128)(4,1)S(1)} %iota_compare_fusion.14, f32[128,512]{1,0:T(8,128)S(1)} %get-tuple-element.297, s32[4096]{0:T(1024)S(1)} %bitcast.207), kind=kOutput, calls=%fused_computation.8.clone.1 | convolution fusion | flops 3224363008 | bytes 573440 | tf_op jit(solution)/shard_map/while/body/eval_jaxpr/dot_general | solution.py:69
  17.4 0.7 dynamic_slice.43
  18.9 3.1 %select_reduce_fusion.4 = f32[2,4096]{1,0:T(2,128)S(1)} fusion(pred[64,4096]{1,0:T(8,128)(4,1)S(1)} %iota_compare_fusion.14, f32[128,512]{1,0:T(8,128)S(1)} %get-tuple-element.297, s32[4096]{0:T(1024)S(1)} %bitcast.207), kind=kOutput, calls=%fused_computation.8.clone.1 | convolution fusion | flops 3224363008 | bytes 573440 | tf_op jit(solution)/shard_map/while/body/eval_jaxpr/dot_general | solution.py:69
  22.0 0.7 dynamic_slice.43
  23.5 3.1 %select_reduce_fusion.4 = f32[2,4096]{1,0:T(2,128)S(1)} fusion(pred[64,4096]{1,0:T(8,128)(4,1)S(1)} %iota_compare_fusion.14, f32[128,512]{1,0:T(8,128)S(1)} %get-tuple-element.297, s32[4096]{0:T(1024)S(1)} %bitcast.207), kind=kOutput, calls=%fused_computation.8.clone.1 | convolution fusion | flops 3224363008 | bytes 573440 | tf_op jit(solution)/shard_map/while/body/eval_jaxpr/dot_general | solution.py:69
  26.7 0.7 dynamic_slice.43
  28.2 3.1 %select_reduce_fusion.4 = f32[2,4096]{1,0:T(2,128)S(1)} fusion(pred[64,4096]{1,0:T(8,128)(4,1)S(1)} %iota_compare_fusion.14, f32[128,512]{1,0:T(8,128)S(1)} %get-tuple-element.297, s32[4096]{0:T(1024)S(1)} %bitcast.207), kind=kOutput, calls=%fused_computation.8.clone.1 | convolution fusion | flops 3224363008 | bytes 573440 | tf_op jit(solution)/shard_map/while/body/eval_jaxpr/dot_general | solution.py:69
  31.3 0.7 dynamic_slice.43
  32.9 3.1 %select_reduce_fusion.4 = f32[2,4096]{1,0:T(2,128)S(1)} fusion(pred[64,4096]{1,0:T(8,128)(4,1)S(1)} %iota_compare_fusion.14, f32[128,512]{1,0:T(8,128)S(1)} %get-tuple-element.297, s32[4096]{0:T(1024)S(1)} %bitcast.207), kind=kOutput, calls=%fused_computation.8.clone.1 | convolution fusion | flops 3224363008 | bytes 573440 | tf_op jit(solution)/shard_map/while/body/eval_jaxpr/dot_general | solution.py:69
  36.0 0.7 dynamic_slice.43
  37.5 3.1 %select_reduce_fusion.4 = f32[2,4096]{1,0:T(2,128)S(1)} fusion(pred[64,4096]{1,0:T(8,128)(4,1)S(1)} %iota_compare_fusion.14, f32[128,512]{1,0:T(8,128)S(1)} %get-tuple-element.297, s32[4096]{0:T(1024)S(1)} %bitcast.207), kind=kOutput, calls=%fused_computation.8.clone.1 | convolution fusion | flops 3224363008 | bytes 573440 | tf_op jit(solution)/shard_map/while/body/eval_jaxpr/dot_general | solution.py:69
  40.7 0.7 dynamic_slice.43
  42.2 3.1 %select_reduce_fusion.4 = f32[2,4096]{1,0:T(2,128)S(1)} fusion(pred[64,4096]{1,0:T(8,128)(4,1)S(1)} %iota_compare_fusion.14, f32[128,512]{1,0:T(8,128)S(1)} %get-tuple-element.297, s32[4096]{0:T(1024)S(1)} %bitcast.207), kind=kOutput, calls=%fused_computation.8.clone.1 | convolution fusion | flops 3224363008 | bytes 573440 | tf_op jit(solution)/shard_map/while/body/eval_jaxpr/dot_general | solution.py:69
  45.3 0.7 dynamic_slice.43
  46.8 3.1 %select_reduce_fusion.4 = f32[2,4096]{1,0:T(2,128)S(1)} fusion(pred[64,4096]{1,0:T(8,128)(4,1)S(1)} %iota_compare_fusion.14, f32[128,512]{1,0:T(8,128)S(1)} %get-tuple-element.297, s32[4096]{0:T(1024)S(1)} %bitcast.207), kind=kOutput, calls=%fused_computation.8.clone.1 | convolution fusion | flops 3224363008 | bytes 573440 | tf_op jit(solution)/shard_map/while/body/eval_jaxpr/dot_general | solution.py:69
  50.0 0.7 dynamic_slice.43
  51.5 3.1 %select_reduce_fusion.4 = f32[2,4096]{1,0:T(2,128)S(1)} fusion(pred[64,4096]{1,0:T(8,128)(4,1)S(1)} %iota_compare_fusion.14, f32[128,512]{1,0:T(8,128)S(1)} %get-tuple-element.297, s32[4096]{0:T(1024)S(1)} %bitcast.207), kind=kOutput, calls=%fused_computation.8.clone.1 | convolution fusion | flops 3224363008 | bytes 573440 | tf_op jit(solution)/shard_map/while/body/eval_jaxpr/dot_general | solution.py:69
  54.6 0.7 dynamic_slice.43
  56.2 3.1 %select_reduce_fusion.4 = f32[2,4096]{1,0:T(2,128)S(1)} fusion(pred[64,4096]{1,0:T(8,128)(4,1)S(1)} %iota_compare_fusion.14, f32[128,512]{1,0:T(8,128)S(1)} %get-tuple-element.297, s32[4096]{0:T(1024)S(1)} %bitcast.207), kind=kOutput, calls=%fused_computation.8.clone.1 | convolution fusion | flops 3224363008 | bytes 573440 | tf_op jit(solution)/shard_map/while/body/eval_jaxpr/dot_general | solution.py:69
  59.3 0.7 dynamic_slice.43
  60.8 3.1 %select_reduce_fusion.4 = f32[2,4096]{1,0:T(2,128)S(1)} fusion(pred[64,4096]{1,0:T(8,128)(4,1)S(1)} %iota_compare_fusion.14, f32[128,512]{1,0:T(8,128)S(1)} %get-tuple-element.297, s32[4096]{0:T(1024)S(1)} %bitcast.207), kind=kOutput, calls=%fused_computation.8.clone.1 | convolution fusion | flops 3224363008 | bytes 573440 | tf_op jit(solution)/shard_map/while/body/eval_jaxpr/dot_general | solution.py:69
  64.0 0.7 dynamic_slice.43
  65.3 0.7 copy-done.1
  87.8 6.2 %all-to-all-start = ((f32[32,2,1,4096]{3,1,2,0:T(2,128)}), f32[32,2,1,4096]{3,1,2,0:T(2,128)S(1)}, u32[]{:S(2)}, u32[]{:S(2)}) async-start(f32[32,2,1,4096]{3,1,2,0:T(2,128)} %constant_dynamic-update-slice_fusion.2), calls=%async_computation | async-start | bytes 2097152 | tf_op jit(solution)/shard_map/all_to_all | solution.py:90
  94.1 1.7 constant_dynamic-update-slice_fusion.1
  95.8 1.0 mul.126
  96.8 1.9 constant_dynamic-update-slice_fusion
  98.7 3.8 %multiply_add_fusion = f32[2,8,64,514]{3,2,1,0:T(8,128)S(1)} fusion(f32[2,8,64,514]{3,2,1,0:T(8,128)} %constant_dynamic-update-slice_fusion, f32[2,8,64,2]{3,2,1,0:T(8,128)} %collective-permute-done.1, f32[2,8,64,512]{3,2,1,0:T(8,128)S(1)} %copy-done, f32[2,8,64,2]{3,2,1,0:T(8,128)} %collective-permute-done, f32[8,64]{1,0:T(8,128)S(1)} %get-tuple-element.201, ...), kind=kLoop, calls=%fused_computation.30 | loop fusion | flops 5789696 | bytes 6328320 | tf_op jit(solution)/shard_map/add | solution.py:28
  103.2 1.3 multiply_add_fusion.1
  104.8 2.6 %pad_subtract_fusion.1 = f32[2,8,64,512]{3,2,1,0:T(8,128)} fusion(f32[2,7,64,512]{3,2,1,0:T(8,128)S(1)} %fusion.17, f32[8,64]{1,0:T(8,128)S(1)} %get-tuple-element.201, f32[2,8,64,514]{3,2,1,0:T(8,128)S(1)} %pad_subtract_fusion, f32[8,64]{1,0:T(8,128)S(1)} %get-tuple-element.200), kind=kLoop, calls=%fused_computation.33 | loop fusion | flops 5242880 | bytes 10227712 | tf_op jit(solution)/shard_map/sub | solution.py:38
  107.4 13.9 %all-to-all-done = f32[32,2,1,4096]{3,1,2,0:T(2,128)S(1)} async-done(((f32[32,2,1,4096]{3,1,2,0:T(2,128)}), f32[32,2,1,4096]{3,1,2,0:T(2,128)S(1)}, u32[]{:S(2)}, u32[]{:S(2)}) %all-to-all-start) | async-done | bytes 1048608 | tf_op jit(solution)/shard_map/all_to_all | solution.py:90
  122.0 1.0 select_reduce_fusion.1
  123.6 73.8 %while.24 = (s32[]{:T(128)}, f32[128,512]{1,0:T(8,128)S(1)}, s32[12,4096]{1,0:T(8,128)}, f32[12,2,4096]{2,1,0:T(2,128)S(1)}, s32[12,4096]{1,0:T(8,128)}, /*index=5*/s32[]{:T(128)}, s32[]{:T(128)}) while((s32[]{:T(128)}, f32[128,512]{1,0:T(8,128)S(1)}, s32[12,4096]{1,0:T(8,128)}, f32[12,2,4096]{2,1,0:T(2,128)S(1)}, ...), condition=%wide.region_6.7_spmd.clone, body=%wide.region_5.6_spmd.clone.sunk | while | flops 3224240128 | bytes 5439591 | solution.py:129
  123.6 1.1 constant_dynamic-slice_fusion.7
  125.1 4.7 %fusion.33 = f32[128,512]{1,0:T(8,128)S(1)} fusion(f32[128,4096]{1,0:T(8,128)S(1)} %bitcast.198, s32[4096]{0:T(1024)S(1)} %bitcast.206, f32[128,512]{1,0:T(8,128)S(1)} %get-tuple-element.307, pred[]{:T(512)S(6)} %compare.17), kind=kOutput, calls=%fused_computation.18.clone.1 | convolution fusion | flops 3223453696 | bytes 2637825 | tf_op jit(solution)/shard_map/while/body/eval_jaxpr/dot_general | solution.py:119
  129.8 1.0 constant_dynamic-slice_fusion.7
  131.2 4.7 %fusion.33 = f32[128,512]{1,0:T(8,128)S(1)} fusion(f32[128,4096]{1,0:T(8,128)S(1)} %bitcast.198, s32[4096]{0:T(1024)S(1)} %bitcast.206, f32[128,512]{1,0:T(8,128)S(1)} %get-tuple-element.307, pred[]{:T(512)S(6)} %compare.17), kind=kOutput, calls=%fused_computation.18.clone.1 | convolution fusion | flops 3223453696 | bytes 2637825 | tf_op jit(solution)/shard_map/while/body/eval_jaxpr/dot_general | solution.py:119
  136.0 1.0 constant_dynamic-slice_fusion.7
  137.4 4.7 %fusion.33 = f32[128,512]{1,0:T(8,128)S(1)} fusion(f32[128,4096]{1,0:T(8,128)S(1)} %bitcast.198, s32[4096]{0:T(1024)S(1)} %bitcast.206, f32[128,512]{1,0:T(8,128)S(1)} %get-tuple-element.307, pred[]{:T(512)S(6)} %compare.17), kind=kOutput, calls=%fused_computation.18.clone.1 | convolution fusion | flops 3223453696 | bytes 2637825 | tf_op jit(solution)/shard_map/while/body/eval_jaxpr/dot_general | solution.py:119
  142.1 1.0 constant_dynamic-slice_fusion.7
  143.5 4.7 %fusion.33 = f32[128,512]{1,0:T(8,128)S(1)} fusion(f32[128,4096]{1,0:T(8,128)S(1)} %bitcast.198, s32[4096]{0:T(1024)S(1)} %bitcast.206, f32[128,512]{1,0:T(8,128)S(1)} %get-tuple-element.307, pred[]{:T(512)S(6)} %compare.17), kind=kOutput, calls=%fused_computation.18.clone.1 | convolution fusion | flops 3223453696 | bytes 2637825 | tf_op jit(solution)/shard_map/while/body/eval_jaxpr/dot_general | solution.py:119
  148.3 1.0 constant_dynamic-slice_fusion.7
  149.7 4.7 %fusion.33 = f32[128,512]{1,0:T(8,128)S(1)} fusion(f32[128,4096]{1,0:T(8,128)S(1)} %bitcast.198, s32[4096]{0:T(1024)S(1)} %bitcast.206, f32[128,512]{1,0:T(8,128)S(1)} %get-tuple-element.307, pred[]{:T(512)S(6)} %compare.17), kind=kOutput, calls=%fused_computation.18.clone.1 | convolution fusion | flops 3223453696 | bytes 2637825 | tf_op jit(solution)/shard_map/while/body/eval_jaxpr/dot_general | solution.py:119
  154.4 1.0 constant_dynamic-slice_fusion.7
  155.8 4.7 %fusion.33 = f32[128,512]{1,0:T(8,128)S(1)} fusion(f32[128,4096]{1,0:T(8,128)S(1)} %bitcast.198, s32[4096]{0:T(1024)S(1)} %bitcast.206, f32[128,512]{1,0:T(8,128)S(1)} %get-tuple-element.307, pred[]{:T(512)S(6)} %compare.17), kind=kOutput, calls=%fused_computation.18.clone.1 | convolution fusion | flops 3223453696 | bytes 2637825 | tf_op jit(solution)/shard_map/while/body/eval_jaxpr/dot_general | solution.py:119
  160.6 1.0 constant_dynamic-slice_fusion.7
  161.9 4.7 %fusion.33 = f32[128,512]{1,0:T(8,128)S(1)} fusion(f32[128,4096]{1,0:T(8,128)S(1)} %bitcast.198, s32[4096]{0:T(1024)S(1)} %bitcast.206, f32[128,512]{1,0:T(8,128)S(1)} %get-tuple-element.307, pred[]{:T(512)S(6)} %compare.17), kind=kOutput, calls=%fused_computation.18.clone.1 | convolution fusion | flops 3223453696 | bytes 2637825 | tf_op jit(solution)/shard_map/while/body/eval_jaxpr/dot_general | solution.py:119
  166.7 1.0 constant_dynamic-slice_fusion.7
  168.1 4.7 %fusion.33 = f32[128,512]{1,0:T(8,128)S(1)} fusion(f32[128,4096]{1,0:T(8,128)S(1)} %bitcast.198, s32[4096]{0:T(1024)S(1)} %bitcast.206, f32[128,512]{1,0:T(8,128)S(1)} %get-tuple-element.307, pred[]{:T(512)S(6)} %compare.17), kind=kOutput, calls=%fused_computation.18.clone.1 | convolution fusion | flops 3223453696 | bytes 2637825 | tf_op jit(solution)/shard_map/while/body/eval_jaxpr/dot_general | solution.py:119
  172.9 1.0 constant_dynamic-slice_fusion.7
  174.2 4.7 %fusion.33 = f32[128,512]{1,0:T(8,128)S(1)} fusion(f32[128,4096]{1,0:T(8,128)S(1)} %bitcast.198, s32[4096]{0:T(1024)S(1)} %bitcast.206, f32[128,512]{1,0:T(8,128)S(1)} %get-tuple-element.307, pred[]{:T(512)S(6)} %compare.17), kind=kOutput, calls=%fused_computation.18.clone.1 | convolution fusion | flops 3223453696 | bytes 2637825 | tf_op jit(solution)/shard_map/while/body/eval_jaxpr/dot_general | solution.py:119
  179.0 1.0 constant_dynamic-slice_fusion.7
  180.4 4.7 %fusion.33 = f32[128,512]{1,0:T(8,128)S(1)} fusion(f32[128,4096]{1,0:T(8,128)S(1)} %bitcast.198, s32[4096]{0:T(1024)S(1)} %bitcast.206, f32[128,512]{1,0:T(8,128)S(1)} %get-tuple-element.307, pred[]{:T(512)S(6)} %compare.17), kind=kOutput, calls=%fused_computation.18.clone.1 | convolution fusion | flops 3223453696 | bytes 2637825 | tf_op jit(solution)/shard_map/while/body/eval_jaxpr/dot_general | solution.py:119
  185.2 1.0 constant_dynamic-slice_fusion.7
  186.5 4.7 %fusion.33 = f32[128,512]{1,0:T(8,128)S(1)} fusion(f32[128,4096]{1,0:T(8,128)S(1)} %bitcast.198, s32[4096]{0:T(1024)S(1)} %bitcast.206, f32[128,512]{1,0:T(8,128)S(1)} %get-tuple-element.307, pred[]{:T(512)S(6)} %compare.17), kind=kOutput, calls=%fused_computation.18.clone.1 | convolution fusion | flops 3223453696 | bytes 2637825 | tf_op jit(solution)/shard_map/while/body/eval_jaxpr/dot_general | solution.py:119
  191.3 1.0 constant_dynamic-slice_fusion.7
  192.7 4.7 %fusion.33 = f32[128,512]{1,0:T(8,128)S(1)} fusion(f32[128,4096]{1,0:T(8,128)S(1)} %bitcast.198, s32[4096]{0:T(1024)S(1)} %bitcast.206, f32[128,512]{1,0:T(8,128)S(1)} %get-tuple-element.307, pred[]{:T(512)S(6)} %compare.17), kind=kOutput, calls=%fused_computation.18.clone.1 | convolution fusion | flops 3223453696 | bytes 2637825 | tf_op jit(solution)/shard_map/while/body/eval_jaxpr/dot_general | solution.py:119
  197.5 1.1 add_bitcast_fusion
  198.6 0.7 fusion.18
  (163 shorter events, 38.4 us)
Async XLA Ops:
  0.6 8.7 %slice-start = ((f32[2,8,64,512]{3,2,1,0:T(8,128)}), f32[2,1,64,512]{3,2,1,0:T(8,128)S(1)}, s32[]{:S(2)}) async-start(f32[2,8,64,512]{3,2,1,0:T(8,128)} %param.15), calls=%async_computation.1 | async-start | bytes 524288 | tf_op jit(solution)/shard_map/slice | solution.py:58
  0.6 8.4 %copy-start.5 = (s32[1,1,3,4,4096]{4,3,2,1,0:T(4,128)S(1)}, s32[1,1,3,4,4096]{4,3,2,1,0:T(4,128)}, u32[]{:S(2)}) copy-start(s32[1,1,3,4,4096]{4,3,2,1,0:T(4,128)} %param.21) | copy-start | bytes 589828
  0.7 8.5 %copy-start.11 = (s32[1,1,3,4]{3,1,2,0:T(1,128)S(1)}, s32[1,1,3,4]{3,1,2,0:T(1,128)}, u32[]{:S(2)}) copy-start(s32[1,1,3,4]{3,1,2,0:T(1,128)} %param.20) | copy-start | bytes 148
  0.7 8.6 %copy-start.6 = (s32[1,1,3,4,4096]{4,3,2,1,0:T(4,128)S(1)}, s32[1,1,3,4,4096]{4,3,2,1,0:T(4,128)}, u32[]{:S(2)}) copy-start(s32[1,1,3,4,4096]{4,3,2,1,0:T(4,128)} %param.22) | copy-start | bytes 589828
  3.1 93.7 %collective-permute-start.1 = (f32[2,8,64,2]{3,2,1,0:T(8,128)}, f32[2,8,64,2]{3,2,1,0:T(8,128)}, u32[]{:S(2)}, u32[]{:S(2)}) collective-permute-start(f32[2,8,64,2]{3,2,1,0:T(8,128)} %get-tuple-element.167), channel_id=1, source_target_pairs={{1,0},{2,1},{3,2},{4,3},{5,4},{6,5},{7,6},{0,7},{9,8},{10,9},{11,1... | collective-permute-start | bytes 24584 | tf_op jit(solution)/shard_map/ppermute | solution.py:18
  9.1 89.7 %collective-permute-start = (f32[2,8,64,2]{3,2,1,0:T(8,128)}, f32[2,8,64,2]{3,2,1,0:T(8,128)}, u32[]{:S(2)}, u32[]{:S(2)}) collective-permute-start(f32[2,8,64,2]{3,2,1,0:T(8,128)} %get-tuple-element.166), channel_id=1, source_target_pairs={{0,1},{1,2},{2,3},{3,4},{4,5},{5,6},{6,7},{7,0},{8,9},{9,10},{10,1... | collective-permute-start | bytes 24584 | tf_op jit(solution)/shard_map/ppermute | solution.py:15
  65.3 0.7 copy-start.1
  65.3 2.4 %copy-start.2 = (s32[12,4096]{1,0:T(8,128)}, s32[12,4096]{1,0:T(8,128)S(1)}, u32[]{:S(2)}) copy-start(s32[12,4096]{1,0:T(8,128)S(1)} %get-tuple-element.322) | copy-start | bytes 589828
  68.4 25.7 %copy-start.10 = (f32[8,64]{1,0:T(8,128)S(1)}, f32[8,64]{1,0:T(8,128)}, u32[]{:S(2)}) copy-start(f32[8,64]{1,0:T(8,128)} %param.16) | copy-start | bytes 6148
  68.4 25.7 %copy-start = (f32[2,8,64,512]{3,2,1,0:T(8,128)S(1)}, f32[2,8,64,512]{3,2,1,0:T(8,128)}, u32[]{:S(2)}) copy-start(f32[2,8,64,512]{3,2,1,0:T(8,128)} %param.15) | copy-start | bytes 6291460
  87.8 33.5 %all-to-all-start = ((f32[32,2,1,4096]{3,1,2,0:T(2,128)}), f32[32,2,1,4096]{3,1,2,0:T(2,128)S(1)}, u32[]{:S(2)}, u32[]{:S(2)}) async-start(f32[32,2,1,4096]{3,1,2,0:T(2,128)} %constant_dynamic-update-slice_fusion.2), calls=%async_computation | async-start | bytes 2097152 | tf_op jit(solution)/shard_map/all_to_all | solution.py:90
  98.7 3.8 %copy-start.9 = (f32[7,64]{1,0:T(8,128)S(1)}, f32[7,64]{1,0:T(8,128)}, u32[]{:S(2)}) copy-start(f32[7,64]{1,0:T(8,128)} %param.17) | copy-start | bytes 5380
  122.0 1.6 copy-start.3
  123.6 73.9 %copy-start.7 = (f32[64,512]{1,0:T(8,128)S(1)}, f32[64,512]{1,0:T(8,128)}, u32[]{:S(2)}) copy-start(f32[64,512]{1,0:T(8,128)} %param.18) | copy-start | bytes 393220
  123.6 73.9 %copy-start.8 = (s32[64,512]{1,0:T(8,128)S(1)}, s32[64,512]{1,0:T(8,128)}, u32[]{:S(2)}) copy-start(s32[64,512]{1,0:T(8,128)} %param.19) | copy-start | bytes 393220
  197.4 1.9 copy-start.4
